TPU v7x, 256 devices: a whole 4x4x8 slice. The times are simulated.
256 devices in a mesh: dp: 4 (over z_lo, core), ang: 4 (over y), rows: 16 (over z_hi, x).
Axes of the slice: x: 4, y: 4, z: 8 (z_hi: 4, z_lo: 2; z = z_hi * 2 + z_lo), core: 2. Of those that a mesh axis runs over, the one named last changes fastest.
Arguments:
- light_field: bfloat16 [4, 1, 8, 64, 64, 512], P('dp', None, 'ang', 'rows'), may hold values from -6 to 6
- spatial_weight: bfloat16 [3, 3, 64, 64], replicated, may hold values from -0.25 to 0.25
- epi_weight: bfloat16 [3, 3, 64, 64], replicated, may hold values from -0.25 to 0.25
- upsample_weight: bfloat16 [16, 64], replicated, may hold values from -0.75 to 0.75
- image_grad: bfloat16 [4, 1, 8, 256, 2048], P('dp', None, 'ang', 'rows'), may hold values from -0.005859375 to 0.005859375
Outputs:
- upscaled: bfloat16 [4, 1, 8, 256, 2048], P('dp', None, 'ang', 'rows')
- spatial_grad: float32 [3, 3, 64, 64], replicated
- epi_grad: float32 [3, 3, 64, 64], replicated
- upsample_grad: float32 [16, 64], replicated
All inputs are finite; a program needn't handle non-finite values.
Results may differ from a plain program's by a relative error of at most 0.0066.
Values may be sent and summed in bfloat16 or wider, within the bound.
No kernel may reach another device: no remote copies, remote signals or barrier semaphores. Data moves between devices by JAX's collectives and lax.ppermute only.
A program may use at most 64 MiB of HBM per device.

v0:
```python
import jax
import jax.numpy as jnp
from jax import lax
from jax.sharding import PartitionSpec as P

SCALE = 4
SUB = 16


def with_halo(cells, sides, width):
    for axis, dim in sides:
        count = lax.axis_size(axis)
        ends = count - 1
        head = lax.slice_in_dim(cells, 0, width, axis=dim)
        tail = lax.slice_in_dim(cells, cells.shape[dim] - width, cells.shape[dim], axis=dim)
        cells = jnp.concatenate(
            [
                lax.ppermute(tail, axis, [(i, (i + 1) % count) for i in range(ends)]),
                cells,
                lax.ppermute(head, axis, [((i + 1) % count, i) for i in range(ends)]),
            ],
            axis=dim,
        )
    return cells


def silu_slope(values):
    sigmoid_value = jax.nn.sigmoid(values)
    return sigmoid_value * (1.0 + values * (1.0 - sigmoid_value))


def spatial_conv(padded, weight, height, breadth):
    summed = jnp.zeros(padded.shape[:3] + (height, weight.shape[2], breadth), jnp.float32)
    for tap_row in range(3):
        for tap_col in range(3):
            summed = summed + jnp.einsum(
                "oc,buvhcw->buvhow",
                weight[tap_row, tap_col],
                padded[:, :, :, tap_row : tap_row + height, :, tap_col : tap_col + breadth],
                preferred_element_type=jnp.float32,
            )
    return summed


def epi_conv(padded, weight, views_all, breadth):
    summed = jnp.zeros(
        padded.shape[:2] + (views_all, padded.shape[3], weight.shape[2], breadth), jnp.float32
    )
    for tap_row in range(3):
        for tap_col in range(3):
            summed = summed + jnp.einsum(
                "oc,buvhcw->buvhow",
                weight[tap_row, tap_col],
                padded[:, :, tap_row : tap_row + views_all, :, :, tap_col : tap_col + breadth],
                preferred_element_type=jnp.float32,
            )
    return summed


def epi_back(padded, weight, views_all, breadth):
    summed = jnp.zeros(
        padded.shape[:2] + (views_all, padded.shape[3], weight.shape[3], breadth), jnp.float32
    )
    for tap_row in range(3):
        for tap_col in range(3):
            summed = summed + jnp.einsum(
                "oc,buvhow->buvhcw",
                weight[tap_row, tap_col],
                padded[
                    :,
                    :,
                    2 - tap_row : 2 - tap_row + views_all,
                    :,
                    :,
                    2 - tap_col : 2 - tap_col + breadth,
                ],
                preferred_element_type=jnp.float32,
            )
    return summed


def weight_grad(upstream, padded, along_dim, extent, breadth):
    rows_out = []
    for tap_row in range(3):
        row_list = []
        for tap_col in range(3):
            window = lax.slice_in_dim(padded, tap_row, tap_row + extent, axis=along_dim)
            window = lax.slice_in_dim(window, tap_col, tap_col + breadth, axis=5)
            row_list.append(
                jnp.einsum(
                    "buvhow,buvhcw->oc", upstream, window, preferred_element_type=jnp.float32
                )
            )
        rows_out.append(jnp.stack(row_list))
    return jnp.stack(rows_out)


def project_up(weight, features):
    return jnp.einsum(
        "sc,buvhcw->buvhsw", weight, features, preferred_element_type=jnp.float32
    ).astype(jnp.bfloat16)


def shift_pairs(kind, step):
    if kind == "x":
        return ("rows", [(g * 4 + i, g * 4 + (i + step) % 4) for g in range(4) for i in range(4)])
    if kind == "z":
        return ("rows", [(4 * i + g, 4 * ((i + step) % 4) + g) for g in range(4) for i in range(4)])
    return (kind, [(i, (i + step) % 4) for i in range(4)])


def place_in(kind):
    if kind == "x":
        return lax.axis_index("rows") % 4
    if kind == "z":
        return lax.axis_index("rows") // 4
    return lax.axis_index(kind)


def shifted(value, kind, step):
    axis, pairs = shift_pairs(kind, step)
    return lax.ppermute(value, axis, pairs)


def gather_sum(value, kind):
    one, two, three = (shifted(value, kind, step) for step in (1, 2, 3))
    return value + two + (one + three)


def scatter_sum(value, kind):
    place = place_in(kind)
    mine = lax.dynamic_index_in_dim(value, place, 0, keepdims=False)
    one, two, three = (
        shifted(lax.dynamic_index_in_dim(value, (place + step) % 4, 0, keepdims=False), kind, step)
        for step in (1, 2, 3)
    )
    return mine + two + (one + three)


def gather_parts(value, kind):
    place = place_in(kind)
    around = jnp.stack([value] + [shifted(value, kind, step) for step in (1, 2, 3)])
    return jnp.concatenate(
        [lax.dynamic_index_in_dim(around, (place - part) % 4, 0) for part in range(4)], axis=0
    )


def sum_everywhere(parts):
    flat = jnp.concatenate([part.reshape(-1, 128) for part in parts], axis=0)
    rows = flat.shape[0]
    share = -(-rows // 32) * 8
    flat = jnp.pad(flat, ((0, 4 * share - rows), (0, 0))).reshape(4, share, 128)
    mine = scatter_sum(flat, "dp")
    for kind in ("x", "z", "ang"):
        mine = gather_sum(mine, kind)
    flat = gather_parts(mine, "dp").reshape(4 * share, 128)
    results, start = ([], 0)
    for part in parts:
        count = part.size // 128
        results.append(flat[start : start + count].reshape(part.shape))
        start += count
    return results


def on_device(light_field, spatial_weight, epi_weight, upsample_weight, image_grad):
    batch_here, angular_rows, views_here, rows_here, channels, breadth = light_field.shape
    rimmed = with_halo(light_field, (("rows", 3),), 1)
    spatial_in = jnp.pad(rimmed, ((0, 0), (0, 0), (0, 0), (0, 0), (0, 0), (1, 1)))
    spatial_out = spatial_conv(spatial_in, spatial_weight, rows_here, breadth)
    first = (light_field.astype(jnp.float32) + jax.nn.silu(spatial_out)).astype(jnp.bfloat16)
    cotangent = image_grad.reshape(
        batch_here, angular_rows, views_here, rows_here, SCALE, breadth, SCALE
    )
    cotangent = cotangent.transpose(0, 1, 2, 3, 4, 6, 5).reshape(
        batch_here, angular_rows, views_here, rows_here, SUB, breadth
    )
    epi_block = lax.all_to_all(first, "ang", split_axis=3, concat_axis=2, tiled=True)
    views_block = epi_block.shape[2]
    padded_block = jnp.pad(epi_block, ((0, 0), (0, 0), (1, 1), (0, 0), (0, 0), (1, 1)))
    block_out = epi_conv(padded_block, epi_weight, views_block, breadth)
    block_second = (epi_block.astype(jnp.float32) + jax.nn.silu(block_out)).astype(jnp.bfloat16)
    views_all = block_second.shape[2]
    second_views = lax.all_to_all(block_second, "ang", split_axis=2, concat_axis=3, tiled=True)
    lifted_views = project_up(upsample_weight, second_views)
    up_grad = jnp.einsum(
        "buvhsw,buvhcw->sc", cotangent, second_views, preferred_element_type=jnp.float32
    )
    view_grad = jnp.einsum(
        "sc,buvhsw->buvhcw", upsample_weight, cotangent, preferred_element_type=jnp.float32
    ).astype(jnp.bfloat16)
    second_grad = lax.all_to_all(view_grad, "ang", split_axis=3, concat_axis=2, tiled=True)
    epi_slope = (second_grad.astype(jnp.float32) * silu_slope(block_out)).astype(jnp.bfloat16)
    epi_grad = weight_grad(epi_slope, padded_block, 2, views_all, breadth)
    slope_pad = jnp.pad(epi_slope, ((0, 0), (0, 0), (1, 1), (0, 0), (0, 0), (1, 1)))
    first_grad = (
        second_grad.astype(jnp.float32) + epi_back(slope_pad, epi_weight, views_all, breadth)
    ).astype(jnp.bfloat16)
    first_views = lax.all_to_all(first_grad, "ang", split_axis=2, concat_axis=3, tiled=True)
    upscaled = lifted_views.reshape(
        batch_here, angular_rows, views_here, rows_here, SCALE, SCALE, breadth
    )
    upscaled = upscaled.transpose(0, 1, 2, 3, 4, 6, 5).reshape(
        batch_here, angular_rows, views_here, rows_here * SCALE, breadth * SCALE
    )
    spatial_slope = (first_views.astype(jnp.float32) * silu_slope(spatial_out)).astype(jnp.bfloat16)
    spatial_grad = weight_grad(spatial_slope, spatial_in, 3, rows_here, breadth)
    spatial_grad, epi_grad, up_grad = sum_everywhere((spatial_grad, epi_grad, up_grad))
    return (upscaled, spatial_grad, epi_grad, up_grad)


def solution(mesh):
    placed = (
        P("dp", None, "ang", "rows", None, None),
        P(),
        P(),
        P(),
        P("dp", None, "ang", "rows", None),
    )
    return jax.shard_map(
        on_device,
        mesh=mesh,
        in_specs=placed,
        out_specs=(P("dp", None, "ang", "rows", None), P(), P(), P()),
        check_vma=False,
    )
```

profile of v0, /device:TPU:1, one launch (start us, length us, event | category | flops | bytes accessed | tf_op | source)
XLA Modules:
  0.0 144.1 jit_solution(14145591861268365492)
XLA Ops:
  0.6 1.0 fusion.178
  1.6 4.0 %collective-permute-start = (bf16[1,1,2,1,64,512]{5,4,3,2,1,0:T(8,128)(2,1)S(1)}, bf16[1,1,2,1,64,512]{5,4,3,2,1,0:T(8,128)(2,1)S(1)}, u32[]{:S(2)}, u32[]{:S(2)}) collective-permute-start(bf16[1,1,2,1,64,512]{5,4,3,2,1,0:T(8,128)(2,1)S(1)} %get-tuple-element.14), channel_id=1, source_target_pairs={{0,1},{1,2},{2,3},{3,4},{4,5},{5,6},{6,7},{7,8},{8,9},{9,10},{10,1... | collective-permute-start | bytes 393224 | tf_op jit(solution)/shard_map/ppermute | solution.py:18
  5.6 1.3 collective-permute-start.1
  6.9 10.8 %reshape.280 = bf16[1,1,2,4,4,512,4]{6,5,4,3,2,1,0:T(8,128)(2,1)} reshape(bf16[1,1,2,16,2048]{4,3,2,1,0:T(8,128)(2,1)} %param.9) | data formatting | bytes 262144 | tf_op jit(solution)/shard_map/reshape | solution.py:171
  17.7 3.7 %copy.156 = bf16[1,1,2,4,4,4,512]{6,3,5,4,2,1,0:T(4,128)(2,1)S(1)} copy(bf16[1,1,2,4,4,4,512]{5,6,4,3,2,1,0:T(8,128)(2,1)} %bitcast.472) | data formatting | bytes 262144 | tf_op jit(solution)/shard_map/transpose | solution.py:174
  21.8 0.8 copy.158
  22.6 4.2 %all-to-all-start.2 = ((bf16[1,1,2,4,64,512]{5,4,2,1,0,3:T(8,128)(2,1)}), bf16[1,1,2,4,64,512]{5,4,2,1,0,3:T(8,128)(2,1)S(1)}, u32[]{:S(2)}, u32[]{:S(2)}) async-start(bf16[1,1,2,4,64,512]{5,4,2,1,0,3:T(8,128)(2,1)} %copy.158), calls=%async_computation.2 | async-start | bytes 1048576 | tf_op jit(solution)/shard_map/all_to_all | solution.py:191
  26.8 0.5 fusion.15
  30.1 1.5 %add_convert_fusion.1 = (bf16[1,1,2,4,64,512]{5,4,3,2,1,0:T(8,128)(2,1)S(1)}, f32[1,1,2,4,64,512]{5,4,3,2,1,0:T(8,128)}) fusion(bf16[1,1,2,4,64,512]{5,4,3,2,1,0:T(8,128)(2,1)S(1)} %copy-done.1, f32[2,4,512,64]{2,3,1,0:T(8,128)S(1)} %fusion.113, f32[2,4,512,64]{2,3,1,0:T(8,128)S(1)} %convolution_add_fusion.9, ...), kind=kOutput, calls=%fused_computation.80 | convolution fusion | flops 35913728 | bytes 4734976 | tf_op jit(solution)/shard_map/oc,buvhcw->buvhow/dot_general | solution.py:36
  31.6 0.9 copy.152
  32.4 2.3 %all-to-all-done.2 = bf16[1,1,2,4,64,512]{5,4,2,1,0,3:T(8,128)(2,1)S(1)} async-done(((bf16[1,1,2,4,64,512]{5,4,2,1,0,3:T(8,128)(2,1)}), bf16[1,1,2,4,64,512]{5,4,2,1,0,3:T(8,128)(2,1)S(1)}, u32[]{:S(2)}, u32[]{:S(2)}) %all-to-all-start.2) | async-done | bytes 524320 | tf_op jit(solution)/shard_map/all_to_all | solution.py:191
  34.8 0.8 copy-done.4
  35.6 3.6 %all-to-all-start = ((bf16[1,1,2,4,64,512]{5,4,2,1,0,3:T(8,128)(2,1)}), bf16[1,1,2,4,64,512]{5,4,2,1,0,3:T(8,128)(2,1)S(1)}, u32[]{:S(2)}, u32[]{:S(2)}) async-start(bf16[1,1,2,4,64,512]{5,4,2,1,0,3:T(8,128)(2,1)} %copy.152), calls=%async_computation | async-start | bytes 1048576 | tf_op jit(solution)/shard_map/all_to_all | solution.py:177
  39.2 2.3 %slice_bitcast_fusion.5 = (bf16[2,4,64,512]{3,2,1,0:T(8,128)(2,1)}, bf16[2,4,64,512]{3,2,1,0:T(8,128)(2,1)}, bf16[2,4,64,512]{3,2,1,0:T(8,128)(2,1)}, bf16[2,4,6...) fusion(bf16[1,1,2,6,64,514]{5,4,3,2,1,0:T(8,128)(2,1)S(1)} %fusion.15), kind=kLoop, calls=%fused_computation.110 | loop fusion | bytes 6291456 | tf_op jit(solution)/shard_map/reshape
  41.7 4.3 %all-to-all-done = bf16[1,1,2,4,64,512]{5,4,2,1,0,3:T(8,128)(2,1)S(1)} async-done(((bf16[1,1,2,4,64,512]{5,4,2,1,0,3:T(8,128)(2,1)}), bf16[1,1,2,4,64,512]{5,4,2,1,0,3:T(8,128)(2,1)S(1)}, u32[]{:S(2)}, u32[]{:S(2)}) %all-to-all-start) | async-done | bytes 524320 | tf_op jit(solution)/shard_map/all_to_all | solution.py:177
  48.6 1.6 %multiply_convert_fusion = (bf16[1,1,8,1,64,512]{5,4,2,3,1,0:T(8,128)(2,1)S(1)}, bf16[1,1,8,1,64,512]{5,4,3,1,0,2:T(8,128)(2,1)}) fusion(f32[1,1,8,1,64,512]{5,4,2,3,1,0:T(8,128)S(1)} %bitcast.475, bf16[1,1,8,1,64,512]{5,4,2,3,1,0:T(8,128)(2,1)S(1)} %bitcast.461, f32[8,512,64]{1,2,0:T(8,128)S(1)} %convolution_add_fusion.1, ...), kind=kOutput, calls=%fused_computation.77 | convolution fusion | flops 37224448 | bytes 4210688 | tf_op jit(solution)/shard_map/oc,buvhcw->buvhow/dot_general | solution.py:51
  54.1 0.4 convolution_add_fusion.20
  54.9 0.4 convolution_add_fusion.18
  56.2 1.3 fusion.8
  57.4 3.5 %all-to-all-start.3 = ((bf16[1,1,8,1,64,512]{5,4,3,1,0,2:T(8,128)(2,1)}), bf16[1,1,8,1,64,512]{5,4,3,1,0,2:T(8,128)(2,1)S(1)}, u32[]{:S(2)}, u32[]{:S(2)}) async-start(bf16[1,1,8,1,64,512]{5,4,3,1,0,2:T(8,128)(2,1)} %fusion.8), calls=%async_computation.3 | async-start | bytes 1048576 | tf_op jit(solution)/shard_map/all_to_all | solution.py:198
  61.5 6.3 %all-to-all-done.3 = bf16[1,1,8,1,64,512]{5,4,3,1,0,2:T(8,128)(2,1)S(1)} async-done(((bf16[1,1,8,1,64,512]{5,4,3,1,0,2:T(8,128)(2,1)}), bf16[1,1,8,1,64,512]{5,4,3,1,0,2:T(8,128)(2,1)S(1)}, u32[]{:S(2)}, u32[]{:S(2)}) %all-to-all-start.3) | async-done | bytes 524320 | tf_op jit(solution)/shard_map/all_to_all | solution.py:198
  67.8 3.5 %all-to-all-start.1 = ((bf16[1,1,8,1,64,512]{5,4,3,1,0,2:T(8,128)(2,1)}), bf16[1,1,8,1,64,512]{5,4,3,1,0,2:T(8,128)(2,1)S(1)}, u32[]{:S(2)}, u32[]{:S(2)}) async-start(bf16[1,1,8,1,64,512]{5,4,3,1,0,2:T(8,128)(2,1)} %get-tuple-element.5), calls=%async_computation.1 | async-start | bytes 1048576 | tf_op jit(solution)/shard_map/all_to_all | solution.py:183
  75.0 3.1 %all-to-all-done.1 = bf16[1,1,8,1,64,512]{5,4,3,1,0,2:T(8,128)(2,1)S(1)} async-done(((bf16[1,1,8,1,64,512]{5,4,3,1,0,2:T(8,128)(2,1)}), bf16[1,1,8,1,64,512]{5,4,3,1,0,2:T(8,128)(2,1)S(1)}, u32[]{:S(2)}, u32[]{:S(2)}) %all-to-all-start.1) | async-done | bytes 524320 | tf_op jit(solution)/shard_map/all_to_all | solution.py:183
  78.6 1.7 %collective-permute-start.2 = (f32[152,128]{1,0:T(8,128)S(1)}, f32[152,128]{1,0:T(8,128)S(1)}, u32[]{:S(2)}, u32[]{:S(2)}) collective-permute-start(f32[152,128]{1,0:T(8,128)S(1)} %get-tuple-element.24), channel_id=1, source_target_pairs={{0,128},{64,192},{128,0},{192,64},{1,129},{65,193},{129,1},{193,65... | collective-permute-start | bytes 233480 | tf_op jit(solution)/shard_map/ppermute | solution.py:122
  80.3 6.1 %collective-permute-start.3 = (f32[152,128]{1,0:T(8,128)S(1)}, f32[152,128]{1,0:T(8,128)S(1)}, u32[]{:S(2)}, u32[]{:S(2)}) collective-permute-start(f32[152,128]{1,0:T(8,128)S(1)} %get-tuple-element.23), channel_id=1, source_target_pairs={{0,64},{64,128},{128,192},{192,0},{1,65},{65,129},{129,193},{193,1... | collective-permute-start | bytes 233480 | tf_op jit(solution)/shard_map/ppermute | solution.py:122
  86.5 1.8 %collective-permute-done.3 = f32[152,128]{1,0:T(8,128)S(1)} collective-permute-done((f32[152,128]{1,0:T(8,128)S(1)}, f32[152,128]{1,0:T(8,128)S(1)}, u32[]{:S(2)}, u32[]{:S(2)}) %collective-permute-start.3) | collective-permute-done | bytes 77856 | tf_op jit(solution)/shard_map/ppermute | solution.py:122
  88.3 2.1 %collective-permute-done.4 = f32[152,128]{1,0:T(8,128)S(1)} collective-permute-done((f32[152,128]{1,0:T(8,128)S(1)}, f32[152,128]{1,0:T(8,128)S(1)}, u32[]{:S(2)}, u32[]{:S(2)}) %collective-permute-start.4) | collective-permute-done | bytes 77856 | tf_op jit(solution)/shard_map/ppermute | solution.py:122
  90.5 3.7 %collective-permute-start.5 = (f32[152,128]{1,0:T(8,128)S(1)}, f32[152,128]{1,0:T(8,128)S(1)}, u32[]{:S(2)}, u32[]{:S(2)}) collective-permute-start(f32[152,128]{1,0:T(8,128)S(1)} %fusion.85), channel_id=1, source_target_pairs={{0,2},{1,3},{2,0},{3,1},{4,6},{5,7},{6,4},{7,5},{8,10},{9,11},{10,... | collective-permute-start | bytes 233480 | tf_op jit(solution)/shard_map/ppermute | solution.py:122
  94.1 1.8 %collective-permute-start.6 = (f32[152,128]{1,0:T(8,128)S(1)}, f32[152,128]{1,0:T(8,128)S(1)}, u32[]{:S(2)}, u32[]{:S(2)}) collective-permute-start(f32[152,128]{1,0:T(8,128)S(1)} %fusion.85), channel_id=1, source_target_pairs={{0,1},{1,2},{2,3},{3,0},{4,5},{5,6},{6,7},{7,4},{8,9},{9,10},{10,1... | collective-permute-start | bytes 233480 | tf_op jit(solution)/shard_map/ppermute | solution.py:122
  95.9 0.9 collective-permute-start.7
  96.8 1.8 %collective-permute-done.6 = f32[152,128]{1,0:T(8,128)S(1)} collective-permute-done((f32[152,128]{1,0:T(8,128)S(1)}, f32[152,128]{1,0:T(8,128)S(1)}, u32[]{:S(2)}, u32[]{:S(2)}) %collective-permute-start.6) | collective-permute-done | bytes 77856 | tf_op jit(solution)/shard_map/ppermute | solution.py:122
  98.6 1.0 collective-permute-done.7
  99.7 7.5 %collective-permute-start.10 = (f32[152,128]{1,0:T(8,128)S(1)}, f32[152,128]{1,0:T(8,128)S(1)}, u32[]{:S(2)}, u32[]{:S(2)}) collective-permute-start(f32[152,128]{1,0:T(8,128)S(1)} %add_add_fusion.2), channel_id=1, source_target_pairs={{0,12},{4,0},{8,4},{12,8},{1,13},{5,1},{9,5},{13,9},{2,14},{6,2},{... | collective-permute-start | bytes 233480 | tf_op jit(solution)/shard_map/ppermute | solution.py:122
  107.2 2.2 %collective-permute-start.8 = (f32[152,128]{1,0:T(8,128)S(1)}, f32[152,128]{1,0:T(8,128)S(1)}, u32[]{:S(2)}, u32[]{:S(2)}) collective-permute-start(f32[152,128]{1,0:T(8,128)S(1)} %add_add_fusion.2), channel_id=1, source_target_pairs={{0,8},{4,12},{8,0},{12,4},{1,9},{5,13},{9,1},{13,5},{2,10},{6,14},... | collective-permute-start | bytes 233480 | tf_op jit(solution)/shard_map/ppermute | solution.py:122
  109.4 2.3 %collective-permute-start.9 = (f32[152,128]{1,0:T(8,128)S(1)}, f32[152,128]{1,0:T(8,128)S(1)}, u32[]{:S(2)}, u32[]{:S(2)}) collective-permute-start(f32[152,128]{1,0:T(8,128)S(1)} %add_add_fusion.2), channel_id=1, source_target_pairs={{0,4},{4,8},{8,12},{12,0},{1,5},{5,9},{9,13},{13,1},{2,6},{6,10},{... | collective-permute-start | bytes 233480 | tf_op jit(solution)/shard_map/ppermute | solution.py:122
  111.7 2.8 %collective-permute-done.8 = f32[152,128]{1,0:T(8,128)S(1)} collective-permute-done((f32[152,128]{1,0:T(8,128)S(1)}, f32[152,128]{1,0:T(8,128)S(1)}, u32[]{:S(2)}, u32[]{:S(2)}) %collective-permute-start.8) | collective-permute-done | bytes 77856 | tf_op jit(solution)/shard_map/ppermute | solution.py:122
  114.5 1.5 %collective-permute-done.9 = f32[152,128]{1,0:T(8,128)S(1)} collective-permute-done((f32[152,128]{1,0:T(8,128)S(1)}, f32[152,128]{1,0:T(8,128)S(1)}, u32[]{:S(2)}, u32[]{:S(2)}) %collective-permute-start.9) | collective-permute-done | bytes 77856 | tf_op jit(solution)/shard_map/ppermute | solution.py:122
  116.4 1.2 collective-permute-start.12
  117.6 1.5 %collective-permute-start.13 = (f32[152,128]{1,0:T(8,128)S(1)}, f32[152,128]{1,0:T(8,128)S(1)}, u32[]{:S(2)}, u32[]{:S(2)}) collective-permute-start(f32[152,128]{1,0:T(8,128)S(1)} %add_add_fusion.1), channel_id=1, source_target_pairs={{0,48},{16,0},{32,16},{48,32},{1,49},{17,1},{33,17},{49,33},{2,50}... | collective-permute-start | bytes 233480 | tf_op jit(solution)/shard_map/ppermute | solution.py:122
  119.1 1.9 %collective-permute-done.11 = f32[152,128]{1,0:T(8,128)S(1)} collective-permute-done((f32[152,128]{1,0:T(8,128)S(1)}, f32[152,128]{1,0:T(8,128)S(1)}, u32[]{:S(2)}, u32[]{:S(2)}) %collective-permute-start.11) | collective-permute-done | bytes 77856 | tf_op jit(solution)/shard_map/ppermute | solution.py:122
  121.0 0.7 collective-permute-done.12
  121.7 6.1 %collective-permute-start.14 = (f32[152,128]{1,0:T(8,128)S(1)}, f32[152,128]{1,0:T(8,128)S(1)}, u32[]{:S(2)}, u32[]{:S(2)}) collective-permute-start(f32[152,128]{1,0:T(8,128)S(1)} %add_add_fusion), channel_id=1, source_target_pairs={{0,64},{64,128},{128,192},{192,0},{1,65},{65,129},{129,193},{193,1... | collective-permute-start | bytes 233480 | tf_op jit(solution)/shard_map/ppermute | solution.py:122
  127.9 0.5 collective-permute-start.16
  128.6 3.3 %copy.155 = bf16[1,1,2,4,4,4,512]{5,6,4,3,2,1,0:T(8,128)(2,1)} copy(bf16[1,1,2,4,4,4,512]{6,5,4,3,2,1,0:T(4,128)(2,1)S(1)} %reshape.278) | data formatting | bytes 262144 | tf_op jit(solution)/shard_map/reshape | solution.py:199
  131.9 9.7 %reshape.279 = bf16[1,1,2,16,2048]{4,3,2,1,0:T(8,128)(2,1)} reshape(bf16[1,1,2,4,4,512,4]{6,5,4,3,2,1,0:T(8,128)(2,1)} %bitcast.471) | data formatting | bytes 262144 | tf_op jit(solution)/shard_map/reshape | solution.py:202
  141.8 0.8 reshape.297
  142.6 0.8 reshape.298
  143.4 0.7 reshape.299
  (112 shorter events, 16.2 us)
Async XLA Ops:
  0.6 20.8 %copy-start = (bf16[16,64]{1,0:T(8,128)(2,1)S(1)}, bf16[16,64]{1,0:T(8,128)(2,1)}, u32[]{:S(2)}) copy-start(bf16[16,64]{1,0:T(8,128)(2,1)} %param.8) | copy-start | bytes 6148
  1.6 25.1 %collective-permute-start = (bf16[1,1,2,1,64,512]{5,4,3,2,1,0:T(8,128)(2,1)S(1)}, bf16[1,1,2,1,64,512]{5,4,3,2,1,0:T(8,128)(2,1)S(1)}, u32[]{:S(2)}, u32[]{:S(2)}) collective-permute-start(bf16[1,1,2,1,64,512]{5,4,3,2,1,0:T(8,128)(2,1)S(1)} %get-tuple-element.14), channel_id=1, source_target_pairs={{0,1},{1,2},{2,3},{3,4},{4,5},{5,6},{6,7},{7,8},{8,9},{9,10},{10,1... | collective-permute-start | bytes 393224 | tf_op jit(solution)/shard_map/ppermute | solution.py:18
  5.6 21.2 %collective-permute-start.1 = (bf16[1,1,2,1,64,512]{5,4,3,2,1,0:T(8,128)(2,1)S(1)}, bf16[1,1,2,1,64,512]{5,4,3,2,1,0:T(8,128)(2,1)S(1)}, u32[]{:S(2)}, u32[]{:S(2)}) collective-permute-start(bf16[1,1,2,1,64,512]{5,4,3,2,1,0:T(8,128)(2,1)S(1)} %get-tuple-element.15), channel_id=1, source_target_pairs={{1,0},{2,1},{3,2},{4,3},{5,4},{6,5},{7,6},{8,7},{9,8},{10,9},{11,1... | collective-permute-start | bytes 393224 | tf_op jit(solution)/shard_map/ppermute | solution.py:20
  21.4 5.4 %copy-start.1 = (bf16[1,1,2,4,64,512]{5,4,3,2,1,0:T(8,128)(2,1)S(1)}, bf16[1,1,2,4,64,512]{5,4,3,2,1,0:T(8,128)(2,1)}, u32[]{:S(2)}) copy-start(bf16[1,1,2,4,64,512]{5,4,3,2,1,0:T(8,128)(2,1)} %param.5) | copy-start | bytes 1572868
  21.8 5.6 %copy-start.16 = (bf16[3,3,64,64]{3,2,1,0:T(8,128)(2,1)S(1)}, bf16[3,3,64,64]{3,2,1,0:T(8,128)(2,1)}, u32[]{:S(2)}) copy-start(bf16[3,3,64,64]{3,2,1,0:T(8,128)(2,1)} %param.6) | copy-start | bytes 221188
  22.6 12.2 %all-to-all-start.2 = ((bf16[1,1,2,4,64,512]{5,4,2,1,0,3:T(8,128)(2,1)}), bf16[1,1,2,4,64,512]{5,4,2,1,0,3:T(8,128)(2,1)S(1)}, u32[]{:S(2)}, u32[]{:S(2)}) async-start(bf16[1,1,2,4,64,512]{5,4,2,1,0,3:T(8,128)(2,1)} %copy.158), calls=%async_computation.2 | async-start | bytes 1048576 | tf_op jit(solution)/shard_map/all_to_all | solution.py:191
  27.7 0.8 copy-start.2
  27.7 2.4 %copy-start.8 = (bf16[2,4,64,512]{3,2,1,0:T(8,128)(2,1)}, bf16[2,4,64,512]{3,2,1,0:T(8,128)(2,1)S(1)}, u32[]{:S(2)}) copy-start(bf16[2,4,64,512]{3,2,1,0:T(8,128)(2,1)S(1)} %get-tuple-element.12) | copy-start | bytes 1572868
  34.8 0.8 copy-start.4
  35.6 10.4 %all-to-all-start = ((bf16[1,1,2,4,64,512]{5,4,2,1,0,3:T(8,128)(2,1)}), bf16[1,1,2,4,64,512]{5,4,2,1,0,3:T(8,128)(2,1)S(1)}, u32[]{:S(2)}, u32[]{:S(2)}) async-start(bf16[1,1,2,4,64,512]{5,4,2,1,0,3:T(8,128)(2,1)} %copy.152), calls=%async_computation | async-start | bytes 1048576 | tf_op jit(solution)/shard_map/all_to_all | solution.py:177
  39.2 2.3 %copy-start.5 = (bf16[1,1,2,4,64,512]{5,4,2,1,0,3:T(8,128)(2,1)S(1)}, bf16[1,1,2,4,64,512]{5,4,2,1,0,3:T(8,128)(2,1)}, u32[]{:S(2)}) copy-start(bf16[1,1,2,4,64,512]{5,4,2,1,0,3:T(8,128)(2,1)} %copy-done.4) | copy-start | bytes 1572868
  39.2 6.7 %copy-start.7 = (bf16[3,3,64,64]{3,2,1,0:T(8,128)(2,1)S(1)}, bf16[3,3,64,64]{3,2,1,0:T(8,128)(2,1)}, u32[]{:S(2)}) copy-start(bf16[3,3,64,64]{3,2,1,0:T(8,128)(2,1)} %param.7) | copy-start | bytes 221188
  57.4 10.4 %all-to-all-start.3 = ((bf16[1,1,8,1,64,512]{5,4,3,1,0,2:T(8,128)(2,1)}), bf16[1,1,8,1,64,512]{5,4,3,1,0,2:T(8,128)(2,1)S(1)}, u32[]{:S(2)}, u32[]{:S(2)}) async-start(bf16[1,1,8,1,64,512]{5,4,3,1,0,2:T(8,128)(2,1)} %fusion.8), calls=%async_computation.3 | async-start | bytes 1048576 | tf_op jit(solution)/shard_map/all_to_all | solution.py:198
  61.3 10.0 %copy-start.6 = (f32[1,1,2,4,64,512]{5,4,3,2,1,0:T(8,128)S(1)}, f32[1,1,2,4,64,512]{5,4,3,2,1,0:T(8,128)}, u32[]{:S(2)}) copy-start(f32[1,1,2,4,64,512]{5,4,3,2,1,0:T(8,128)} %get-tuple-element.26) | copy-start | bytes 3145732
  61.3 10.4 %copy-start.3 = (bf16[2,4,64,512]{3,2,1,0:T(8,128)(2,1)S(1)}, bf16[2,4,64,512]{3,2,1,0:T(8,128)(2,1)}, u32[]{:S(2)}) copy-start(bf16[2,4,64,512]{3,2,1,0:T(8,128)(2,1)} %copy-done.2) | copy-start | bytes 1572868
  67.8 10.4 %all-to-all-start.1 = ((bf16[1,1,8,1,64,512]{5,4,3,1,0,2:T(8,128)(2,1)}), bf16[1,1,8,1,64,512]{5,4,3,1,0,2:T(8,128)(2,1)S(1)}, u32[]{:S(2)}, u32[]{:S(2)}) async-start(bf16[1,1,8,1,64,512]{5,4,3,1,0,2:T(8,128)(2,1)} %get-tuple-element.5), calls=%async_computation.1 | async-start | bytes 1048576 | tf_op jit(solution)/shard_map/all_to_all | solution.py:183
  71.3 1.0 copy-start.9
  71.7 1.1 copy-start.15
  72.0 1.1 copy-start.14
  72.3 1.1 copy-start.13
  72.8 1.1 copy-start.12
  73.2 1.1 copy-start.11
  73.5 1.1 copy-start.10
  78.6 7.9 %collective-permute-start.2 = (f32[152,128]{1,0:T(8,128)S(1)}, f32[152,128]{1,0:T(8,128)S(1)}, u32[]{:S(2)}, u32[]{:S(2)}) collective-permute-start(f32[152,128]{1,0:T(8,128)S(1)} %get-tuple-element.24), channel_id=1, source_target_pairs={{0,128},{64,192},{128,0},{192,64},{1,129},{65,193},{129,1},{193,65... | collective-permute-start | bytes 233480 | tf_op jit(solution)/shard_map/ppermute | solution.py:122
  80.3 8.0 %collective-permute-start.3 = (f32[152,128]{1,0:T(8,128)S(1)}, f32[152,128]{1,0:T(8,128)S(1)}, u32[]{:S(2)}, u32[]{:S(2)}) collective-permute-start(f32[152,128]{1,0:T(8,128)S(1)} %get-tuple-element.23), channel_id=1, source_target_pairs={{0,64},{64,128},{128,192},{192,0},{1,65},{65,129},{129,193},{193,1... | collective-permute-start | bytes 233480 | tf_op jit(solution)/shard_map/ppermute | solution.py:122
  86.4 4.1 %collective-permute-start.4 = (f32[152,128]{1,0:T(8,128)S(1)}, f32[152,128]{1,0:T(8,128)S(1)}, u32[]{:S(2)}, u32[]{:S(2)}) collective-permute-start(f32[152,128]{1,0:T(8,128)S(1)} %get-tuple-element.22), channel_id=1, source_target_pairs={{0,192},{64,0},{128,64},{192,128},{1,193},{65,1},{129,65},{193,129... | collective-permute-start | bytes 233480 | tf_op jit(solution)/shard_map/ppermute | solution.py:122
  90.5 6.4 %collective-permute-start.5 = (f32[152,128]{1,0:T(8,128)S(1)}, f32[152,128]{1,0:T(8,128)S(1)}, u32[]{:S(2)}, u32[]{:S(2)}) collective-permute-start(f32[152,128]{1,0:T(8,128)S(1)} %fusion.85), channel_id=1, source_target_pairs={{0,2},{1,3},{2,0},{3,1},{4,6},{5,7},{6,4},{7,5},{8,10},{9,11},{10,... | collective-permute-start | bytes 233480 | tf_op jit(solution)/shard_map/ppermute | solution.py:122
  94.1 4.5 %collective-permute-start.6 = (f32[152,128]{1,0:T(8,128)S(1)}, f32[152,128]{1,0:T(8,128)S(1)}, u32[]{:S(2)}, u32[]{:S(2)}) collective-permute-start(f32[152,128]{1,0:T(8,128)S(1)} %fusion.85), channel_id=1, source_target_pairs={{0,1},{1,2},{2,3},{3,0},{4,5},{5,6},{6,7},{7,4},{8,9},{9,10},{10,1... | collective-permute-start | bytes 233480 | tf_op jit(solution)/shard_map/ppermute | solution.py:122
  95.9 3.7 %collective-permute-start.7 = (f32[152,128]{1,0:T(8,128)S(1)}, f32[152,128]{1,0:T(8,128)S(1)}, u32[]{:S(2)}, u32[]{:S(2)}) collective-permute-start(f32[152,128]{1,0:T(8,128)S(1)} %fusion.85), channel_id=1, source_target_pairs={{0,3},{1,0},{2,1},{3,2},{4,7},{5,4},{6,5},{7,6},{8,11},{9,8},{10,9... | collective-permute-start | bytes 233480 | tf_op jit(solution)/shard_map/ppermute | solution.py:122
  99.7 12.0 %collective-permute-start.10 = (f32[152,128]{1,0:T(8,128)S(1)}, f32[152,128]{1,0:T(8,128)S(1)}, u32[]{:S(2)}, u32[]{:S(2)}) collective-permute-start(f32[152,128]{1,0:T(8,128)S(1)} %add_add_fusion.2), channel_id=1, source_target_pairs={{0,12},{4,0},{8,4},{12,8},{1,13},{5,1},{9,5},{13,9},{2,14},{6,2},{... | collective-permute-start | bytes 233480 | tf_op jit(solution)/shard_map/ppermute | solution.py:122
  107.2 7.3 %collective-permute-start.8 = (f32[152,128]{1,0:T(8,128)S(1)}, f32[152,128]{1,0:T(8,128)S(1)}, u32[]{:S(2)}, u32[]{:S(2)}) collective-permute-start(f32[152,128]{1,0:T(8,128)S(1)} %add_add_fusion.2), channel_id=1, source_target_pairs={{0,8},{4,12},{8,0},{12,4},{1,9},{5,13},{9,1},{13,5},{2,10},{6,14},... | collective-permute-start | bytes 233480 | tf_op jit(solution)/shard_map/ppermute | solution.py:122
  109.4 6.6 %collective-permute-start.9 = (f32[152,128]{1,0:T(8,128)S(1)}, f32[152,128]{1,0:T(8,128)S(1)}, u32[]{:S(2)}, u32[]{:S(2)}) collective-permute-start(f32[152,128]{1,0:T(8,128)S(1)} %add_add_fusion.2), channel_id=1, source_target_pairs={{0,4},{4,8},{8,12},{12,0},{1,5},{5,9},{9,13},{13,1},{2,6},{6,10},{... | collective-permute-start | bytes 233480 | tf_op jit(solution)/shard_map/ppermute | solution.py:122
  116.0 4.9 %collective-permute-start.11 = (f32[152,128]{1,0:T(8,128)S(1)}, f32[152,128]{1,0:T(8,128)S(1)}, u32[]{:S(2)}, u32[]{:S(2)}) collective-permute-start(f32[152,128]{1,0:T(8,128)S(1)} %add_add_fusion.1), channel_id=1, source_target_pairs={{0,32},{16,48},{32,0},{48,16},{1,33},{17,49},{33,1},{49,17},{2,34}... | collective-permute-start | bytes 233480 | tf_op jit(solution)/shard_map/ppermute | solution.py:122
  116.4 5.3 %collective-permute-start.12 = (f32[152,128]{1,0:T(8,128)S(1)}, f32[152,128]{1,0:T(8,128)S(1)}, u32[]{:S(2)}, u32[]{:S(2)}) collective-permute-start(f32[152,128]{1,0:T(8,128)S(1)} %add_add_fusion.1), channel_id=1, source_target_pairs={{0,16},{16,32},{32,48},{48,0},{1,17},{17,33},{33,49},{49,1},{2,18}... | collective-permute-start | bytes 233480 | tf_op jit(solution)/shard_map/ppermute | solution.py:122
  117.6 4.1 %collective-permute-start.13 = (f32[152,128]{1,0:T(8,128)S(1)}, f32[152,128]{1,0:T(8,128)S(1)}, u32[]{:S(2)}, u32[]{:S(2)}) collective-permute-start(f32[152,128]{1,0:T(8,128)S(1)} %add_add_fusion.1), channel_id=1, source_target_pairs={{0,48},{16,0},{32,16},{48,32},{1,49},{17,1},{33,17},{49,33},{2,50}... | collective-permute-start | bytes 233480 | tf_op jit(solution)/shard_map/ppermute | solution.py:122
  121.7 19.9 %collective-permute-start.14 = (f32[152,128]{1,0:T(8,128)S(1)}, f32[152,128]{1,0:T(8,128)S(1)}, u32[]{:S(2)}, u32[]{:S(2)}) collective-permute-start(f32[152,128]{1,0:T(8,128)S(1)} %add_add_fusion), channel_id=1, source_target_pairs={{0,64},{64,128},{128,192},{192,0},{1,65},{65,129},{129,193},{193,1... | collective-permute-start | bytes 233480 | tf_op jit(solution)/shard_map/ppermute | solution.py:122
  127.9 13.7 %collective-permute-start.15 = (f32[152,128]{1,0:T(8,128)S(1)}, f32[152,128]{1,0:T(8,128)S(1)}, u32[]{:S(2)}, u32[]{:S(2)}) collective-permute-start(f32[152,128]{1,0:T(8,128)S(1)} %add_add_fusion), channel_id=1, source_target_pairs={{0,128},{64,192},{128,0},{192,64},{1,129},{65,193},{129,1},{193,65... | collective-permute-start | bytes 233480 | tf_op jit(solution)/shard_map/ppermute | solution.py:122
  127.9 13.7 %collective-permute-start.16 = (f32[152,128]{1,0:T(8,128)S(1)}, f32[152,128]{1,0:T(8,128)S(1)}, u32[]{:S(2)}, u32[]{:S(2)}) collective-permute-start(f32[152,128]{1,0:T(8,128)S(1)} %add_add_fusion), channel_id=1, source_target_pairs={{0,192},{64,0},{128,64},{192,128},{1,193},{65,1},{129,65},{193,129... | collective-permute-start | bytes 233480 | tf_op jit(solution)/shard_map/ppermute | solution.py:122
where the time goes:
time: 145 us; the launch traced here: 144 us
  starting transfers between devices  56 us (39%)
  local copies, waits for them, and re-layouts  36.7 us (25%)
  waiting for transfers between devices  29.8 us (21%)
  matrix products  18.9 us (13%)
    ppermute x15, starting transfers between devices, shifted(): return lax.ppermute(value, axis, pairs)  35.9 us
    ppermute x15, waiting for transfers between devices, shifted(): return lax.ppermute(value, axis, pairs)  13.7 us
    reshape x1, local copies, waits for them, and re-layouts, on_device(): image_grad.reshape(batch_here, angular_rows, views_here, rows_here, SCALE...  10.8 us
    reshape x1, local copies, waits for them, and re-layouts, on_device(): upscaled.transpose(0, 1, 2, 3, 4, 6, 5)  9.74 us
    all_to_all x1, waiting for transfers between devices, on_device(): lax.all_to_all(first_grad, 'ang', split_axis=2, concat_axis=3, tiled=True)  6.33 us
    dot_general x18, matrix products, weight_grad(): jnp.einsum('buvhow,buvhcw->oc', upstream, window, preferred_element_type=...  5.51 us
    dot_general x9, matrix products, epi_back(): jnp.einsum('oc,buvhow->buvhcw', weight[tap_row, tap_col], padded[:, :, 2...  4.45 us
    all_to_all x1, waiting for transfers between devices, on_device(): lax.all_to_all(first, 'ang', split_axis=3, concat_axis=2, tiled=True)  4.28 us
  transfers between devices with their start and end apart: 21, of which 12 were waited for; matrix products, arithmetic and copies ran while one was open for 28% of the time, Pallas kernels for 0%

commit v1 on v0

--- a/solution.py
+++ b/solution.py
@@ -188,7 +188,10 @@
     view_grad = jnp.einsum(
         "sc,buvhsw->buvhcw", upsample_weight, cotangent, preferred_element_type=jnp.float32
     ).astype(jnp.bfloat16)
-    second_grad = lax.all_to_all(view_grad, "ang", split_axis=3, concat_axis=2, tiled=True)
+    second_grad = jnp.concatenate(
+        lax.all_to_all(jnp.stack(jnp.split(view_grad, lax.axis_size("ang"), axis=3)), "ang", 0, 0),
+        axis=2,
+    )
     epi_slope = (second_grad.astype(jnp.float32) * silu_slope(block_out)).astype(jnp.bfloat16)
     epi_grad = weight_grad(epi_slope, padded_block, 2, views_all, breadth)
     slope_pad = jnp.pad(epi_slope, ((0, 0), (0, 0), (1, 1), (0, 0), (0, 0), (1, 1)))

time: 145 us -> 149 us (1.028)
  matrix products: 18.9 us -> 22.7 us
  local copies, waits for them, and re-layouts: 36.7 us -> 35 us
    dot_general x9, matrix products: 4.24 us -> 6.5 us  [epi_conv(): jnp.einsum('oc,buvhcw->buvhow', weight[tap_row, tap_col], padded[:, :, ta...]
    dot_general x9, matrix products: 3.95 us -> 5.47 us  [spatial_conv(): jnp.einsum('oc,buvhcw->buvhow', weight[tap_row, tap_col], padded[:, :, :,...]
  transfers between devices with their start and end apart: 21 -> 21, of which waited for: 12 -> 12; matrix products, arithmetic and copies ran while one was open for 28% -> 26% of each run, Pallas kernels for 0% -> 0%
where the time goes in v1:
time: 149 us; the launch traced here: 148 us
  starting transfers between devices  56 us (38%)
  local copies, waits for them, and re-layouts  35 us (23%)
  waiting for transfers between devices  31.1 us (21%)
  matrix products  22.7 us (15%)
  other arithmetic  2.17 us (1%)
    ppermute x15, starting transfers between devices, shifted(): return lax.ppermute(value, axis, pairs)  36 us
    ppermute x15, waiting for transfers between devices, shifted(): return lax.ppermute(value, axis, pairs)  13.7 us
    reshape x1, local copies, waits for them, and re-layouts, on_device(): image_grad.reshape(batch_here, angular_rows, views_here, rows_here, SCALE...  10.8 us
    reshape x1, local copies, waits for them, and re-layouts, on_device(): upscaled.transpose(0, 1, 2, 3, 4, 6, 5)  9.74 us
    dot_general x9, matrix products, epi_conv(): jnp.einsum('oc,buvhcw->buvhow', weight[tap_row, tap_col], padded[:, :, ta...  6.5 us
    all_to_all x1, waiting for transfers between devices, on_device(): lax.all_to_all(first_grad, 'ang', split_axis=2, concat_axis=3, tiled=True)  6.33 us
    dot_general x18, matrix products, weight_grad(): jnp.einsum('buvhow,buvhcw->oc', upstream, window, preferred_element_type=...  5.49 us
    dot_general x9, matrix products, spatial_conv(): jnp.einsum('oc,buvhcw->buvhow', weight[tap_row, tap_col], padded[:, :, :,...  5.47 us
  transfers between devices with their start and end apart: 21, of which 12 were waited for; matrix products, arithmetic and copies ran while one was open for 26% of the time, Pallas kernels for 0%

profile of v1, /device:TPU:1, one launch (start us, length us, event | category | flops | bytes accessed | tf_op | source)
XLA Modules:
  0.0 148.3 jit_solution(9038831059442655845)
XLA Ops:
  0.6 1.0 fusion.178
  1.6 4.0 %collective-permute-start = (bf16[1,1,2,1,64,512]{5,4,3,2,1,0:T(8,128)(2,1)S(1)}, bf16[1,1,2,1,64,512]{5,4,3,2,1,0:T(8,128)(2,1)S(1)}, u32[]{:S(2)}, u32[]{:S(2)}) collective-permute-start(bf16[1,1,2,1,64,512]{5,4,3,2,1,0:T(8,128)(2,1)S(1)} %get-tuple-element.18), channel_id=1, source_target_pairs={{0,1},{1,2},{2,3},{3,4},{4,5},{5,6},{6,7},{7,8},{8,9},{9,10},{10,1... | collective-permute-start | bytes 393224 | tf_op jit(solution)/shard_map/ppermute | solution.py:18
  5.6 1.3 collective-permute-start.1
  6.9 10.8 %reshape.279 = bf16[1,1,2,4,4,512,4]{6,5,4,3,2,1,0:T(8,128)(2,1)} reshape(bf16[1,1,2,16,2048]{4,3,2,1,0:T(8,128)(2,1)} %param.9) | data formatting | bytes 262144 | tf_op jit(solution)/shard_map/reshape | solution.py:171
  17.7 3.8 %copy.164 = bf16[1,1,2,4,4,4,512]{6,3,5,4,2,1,0:T(4,128)(2,1)S(1)} copy(bf16[1,1,2,4,4,4,512]{5,6,4,3,2,1,0:T(8,128)(2,1)} %bitcast.482) | data formatting | bytes 262144 | tf_op jit(solution)/shard_map/transpose | solution.py:174
  21.9 0.5 fusion.15
  22.5 1.0 fusion.122
  23.5 1.1 fusion.113
  26.6 1.5 %add_convert_fusion.1 = (bf16[1,1,2,4,64,512]{5,4,3,2,1,0:T(8,128)(2,1)S(1)}, f32[1,1,2,4,64,512]{5,4,3,2,1,0:T(8,128)}) fusion(bf16[1,1,2,4,64,512]{5,4,3,2,1,0:T(8,128)(2,1)S(1)} %copy-done.1, f32[2,4,512,64]{2,3,1,0:T(8,128)S(1)} %fusion.113, f32[2,4,512,64]{2,3,1,0:T(8,128)S(1)} %convolution_add_fusion.9, ...), kind=kOutput, calls=%fused_computation.81 | convolution fusion | flops 35913728 | bytes 4734976 | tf_op jit(solution)/shard_map/oc,buvhcw->buvhow/dot_general | solution.py:36
  28.1 0.9 copy.160
  29.0 4.2 %all-to-all-start = ((bf16[1,1,2,4,64,512]{5,4,2,1,0,3:T(8,128)(2,1)}), bf16[1,1,2,4,64,512]{5,4,2,1,0,3:T(8,128)(2,1)S(1)}, u32[]{:S(2)}, u32[]{:S(2)}) async-start(bf16[1,1,2,4,64,512]{5,4,2,1,0,3:T(8,128)(2,1)} %copy.160), calls=%async_computation | async-start | bytes 1048576 | tf_op jit(solution)/shard_map/all_to_all | solution.py:177
  33.2 0.9 pad_maximum_fusion.2
  34.0 2.3 %slice_bitcast_fusion.5 = (bf16[2,4,64,512]{3,2,1,0:T(8,128)(2,1)}, bf16[2,4,64,512]{3,2,1,0:T(8,128)(2,1)}, bf16[2,4,64,512]{3,2,1,0:T(8,128)(2,1)}, bf16[2,4,6...) fusion(bf16[1,1,2,6,64,514]{5,4,3,2,1,0:T(8,128)(2,1)S(1)} %fusion.15), kind=kLoop, calls=%fused_computation.111 | loop fusion | bytes 6291456 | tf_op jit(solution)/shard_map/reshape
  36.3 4.8 %all-to-all-done = bf16[1,1,2,4,64,512]{5,4,2,1,0,3:T(8,128)(2,1)S(1)} async-done(((bf16[1,1,2,4,64,512]{5,4,2,1,0,3:T(8,128)(2,1)}), bf16[1,1,2,4,64,512]{5,4,2,1,0,3:T(8,128)(2,1)S(1)}, u32[]{:S(2)}, u32[]{:S(2)}) %all-to-all-start) | async-done | bytes 524320 | tf_op jit(solution)/shard_map/all_to_all | solution.py:177
  41.1 3.6 %all-to-all-start.2 = ((bf16[4,1,1,2,1,64,512]{6,5,3,4,2,1,0:T(8,128)(2,1)}), bf16[4,1,1,2,1,64,512]{6,5,3,4,2,1,0:T(8,128)(2,1)S(1)}, u32[]{:S(2)}, u32[]{:S(2)}) async-start(bf16[4,1,1,2,1,64,512]{6,5,3,4,2,1,0:T(8,128)(2,1)} %pad_maximum_fusion.2), calls=%async_computation.2 | async-start | bytes 1048576 | tf_op jit(solution)/shard_map/all_to_all | solution.py:192
  47.2 1.3 convolution_add_fusion.1
  48.5 3.0 %all-to-all-done.2 = bf16[4,1,1,2,1,64,512]{6,5,3,4,2,1,0:T(8,128)(2,1)S(1)} async-done(((bf16[4,1,1,2,1,64,512]{6,5,3,4,2,1,0:T(8,128)(2,1)}), bf16[4,1,1,2,1,64,512]{6,5,3,4,2,1,0:T(8,128)(2,1)S(1)}, u32[]{:S(2)}, u32[]{:S(2)}) %all-to-all-start.2) | async-done | bytes 524320 | tf_op jit(solution)/shard_map/all_to_all | solution.py:192
  51.5 2.9 %fusion.12 = (bf16[1,1,8,1,64,512]{5,4,2,3,1,0:T(8,128)(2,1)S(1)}, bf16[1,1,8,1,64,512]{5,4,3,1,0,2:T(8,128)(2,1)}) fusion(bf16[1,1,8,1,64,512]{5,4,2,3,1,0:T(8,128)(2,1)S(1)} %bitcast.485, bf16[1,1,8,1,64,512]{5,4,2,3,1,0:T(8,128)(2,1)S(1)} %bitcast.471, f32[8,512,64]{1,2,0:T(8,128)} %convolution_add_fusion.1, bf16[3,3,64,64]{3,2,1,0:T(8,128)(2,1)S(1)} %copy-done.3), kind=kOutput, calls=%fused_computation.76 | convolution fusion | flops 37486592 | bytes 3686400 | tf_op jit(solution)/shard_map/oc,buvhcw->buvhow/dot_general | solution.py:51
  60.3 1.3 fusion.7
  61.6 3.5 %all-to-all-start.3 = ((bf16[1,1,8,1,64,512]{5,4,3,1,0,2:T(8,128)(2,1)}), bf16[1,1,8,1,64,512]{5,4,3,1,0,2:T(8,128)(2,1)S(1)}, u32[]{:S(2)}, u32[]{:S(2)}) async-start(bf16[1,1,8,1,64,512]{5,4,3,1,0,2:T(8,128)(2,1)} %fusion.7), calls=%async_computation.3 | async-start | bytes 1048576 | tf_op jit(solution)/shard_map/all_to_all | solution.py:201
  65.7 6.3 %all-to-all-done.3 = bf16[1,1,8,1,64,512]{5,4,3,1,0,2:T(8,128)(2,1)S(1)} async-done(((bf16[1,1,8,1,64,512]{5,4,3,1,0,2:T(8,128)(2,1)}), bf16[1,1,8,1,64,512]{5,4,3,1,0,2:T(8,128)(2,1)S(1)}, u32[]{:S(2)}, u32[]{:S(2)}) %all-to-all-start.3) | async-done | bytes 524320 | tf_op jit(solution)/shard_map/all_to_all | solution.py:201
  72.0 3.5 %all-to-all-start.1 = ((bf16[1,1,8,1,64,512]{5,4,3,1,0,2:T(8,128)(2,1)}), bf16[1,1,8,1,64,512]{5,4,3,1,0,2:T(8,128)(2,1)S(1)}, u32[]{:S(2)}, u32[]{:S(2)}) async-start(bf16[1,1,8,1,64,512]{5,4,3,1,0,2:T(8,128)(2,1)} %get-tuple-element.5), calls=%async_computation.1 | async-start | bytes 1048576 | tf_op jit(solution)/shard_map/all_to_all | solution.py:183
  79.2 3.2 %all-to-all-done.1 = bf16[1,1,8,1,64,512]{5,4,3,1,0,2:T(8,128)(2,1)S(1)} async-done(((bf16[1,1,8,1,64,512]{5,4,3,1,0,2:T(8,128)(2,1)}), bf16[1,1,8,1,64,512]{5,4,3,1,0,2:T(8,128)(2,1)S(1)}, u32[]{:S(2)}, u32[]{:S(2)}) %all-to-all-start.1) | async-done | bytes 524320 | tf_op jit(solution)/shard_map/all_to_all | solution.py:183
  82.8 1.8 %collective-permute-start.2 = (f32[152,128]{1,0:T(8,128)S(1)}, f32[152,128]{1,0:T(8,128)S(1)}, u32[]{:S(2)}, u32[]{:S(2)}) collective-permute-start(f32[152,128]{1,0:T(8,128)S(1)} %get-tuple-element.28), channel_id=1, source_target_pairs={{0,128},{64,192},{128,0},{192,64},{1,129},{65,193},{129,1},{193,65... | collective-permute-start | bytes 233480 | tf_op jit(solution)/shard_map/ppermute | solution.py:122
  84.5 5.9 %collective-permute-start.3 = (f32[152,128]{1,0:T(8,128)S(1)}, f32[152,128]{1,0:T(8,128)S(1)}, u32[]{:S(2)}, u32[]{:S(2)}) collective-permute-start(f32[152,128]{1,0:T(8,128)S(1)} %get-tuple-element.27), channel_id=1, source_target_pairs={{0,64},{64,128},{128,192},{192,0},{1,65},{65,129},{129,193},{193,1... | collective-permute-start | bytes 233480 | tf_op jit(solution)/shard_map/ppermute | solution.py:122
  90.7 1.5 %collective-permute-done.3 = f32[152,128]{1,0:T(8,128)S(1)} collective-permute-done((f32[152,128]{1,0:T(8,128)S(1)}, f32[152,128]{1,0:T(8,128)S(1)}, u32[]{:S(2)}, u32[]{:S(2)}) %collective-permute-start.3) | collective-permute-done | bytes 77856 | tf_op jit(solution)/shard_map/ppermute | solution.py:122
  92.2 2.5 %collective-permute-done.4 = f32[152,128]{1,0:T(8,128)S(1)} collective-permute-done((f32[152,128]{1,0:T(8,128)S(1)}, f32[152,128]{1,0:T(8,128)S(1)}, u32[]{:S(2)}, u32[]{:S(2)}) %collective-permute-start.4) | collective-permute-done | bytes 77856 | tf_op jit(solution)/shard_map/ppermute | solution.py:122
  94.7 3.7 %collective-permute-start.5 = (f32[152,128]{1,0:T(8,128)S(1)}, f32[152,128]{1,0:T(8,128)S(1)}, u32[]{:S(2)}, u32[]{:S(2)}) collective-permute-start(f32[152,128]{1,0:T(8,128)S(1)} %fusion.85), channel_id=1, source_target_pairs={{0,2},{1,3},{2,0},{3,1},{4,6},{5,7},{6,4},{7,5},{8,10},{9,11},{10,... | collective-permute-start | bytes 233480 | tf_op jit(solution)/shard_map/ppermute | solution.py:122
  98.3 1.8 %collective-permute-start.6 = (f32[152,128]{1,0:T(8,128)S(1)}, f32[152,128]{1,0:T(8,128)S(1)}, u32[]{:S(2)}, u32[]{:S(2)}) collective-permute-start(f32[152,128]{1,0:T(8,128)S(1)} %fusion.85), channel_id=1, source_target_pairs={{0,1},{1,2},{2,3},{3,0},{4,5},{5,6},{6,7},{7,4},{8,9},{9,10},{10,1... | collective-permute-start | bytes 233480 | tf_op jit(solution)/shard_map/ppermute | solution.py:122
  100.1 0.9 collective-permute-start.7
  101.0 1.8 %collective-permute-done.6 = f32[152,128]{1,0:T(8,128)S(1)} collective-permute-done((f32[152,128]{1,0:T(8,128)S(1)}, f32[152,128]{1,0:T(8,128)S(1)}, u32[]{:S(2)}, u32[]{:S(2)}) %collective-permute-start.6) | collective-permute-done | bytes 77856 | tf_op jit(solution)/shard_map/ppermute | solution.py:122
  102.8 1.0 collective-permute-done.7
  103.9 7.5 %collective-permute-start.10 = (f32[152,128]{1,0:T(8,128)S(1)}, f32[152,128]{1,0:T(8,128)S(1)}, u32[]{:S(2)}, u32[]{:S(2)}) collective-permute-start(f32[152,128]{1,0:T(8,128)S(1)} %add_add_fusion.2), channel_id=1, source_target_pairs={{0,12},{4,0},{8,4},{12,8},{1,13},{5,1},{9,5},{13,9},{2,14},{6,2},{... | collective-permute-start | bytes 233480 | tf_op jit(solution)/shard_map/ppermute | solution.py:122
  111.4 2.2 %collective-permute-start.8 = (f32[152,128]{1,0:T(8,128)S(1)}, f32[152,128]{1,0:T(8,128)S(1)}, u32[]{:S(2)}, u32[]{:S(2)}) collective-permute-start(f32[152,128]{1,0:T(8,128)S(1)} %add_add_fusion.2), channel_id=1, source_target_pairs={{0,8},{4,12},{8,0},{12,4},{1,9},{5,13},{9,1},{13,5},{2,10},{6,14},... | collective-permute-start | bytes 233480 | tf_op jit(solution)/shard_map/ppermute | solution.py:122
  113.6 2.3 %collective-permute-start.9 = (f32[152,128]{1,0:T(8,128)S(1)}, f32[152,128]{1,0:T(8,128)S(1)}, u32[]{:S(2)}, u32[]{:S(2)}) collective-permute-start(f32[152,128]{1,0:T(8,128)S(1)} %add_add_fusion.2), channel_id=1, source_target_pairs={{0,4},{4,8},{8,12},{12,0},{1,5},{5,9},{9,13},{13,1},{2,6},{6,10},{... | collective-permute-start | bytes 233480 | tf_op jit(solution)/shard_map/ppermute | solution.py:122
  115.9 2.8 %collective-permute-done.8 = f32[152,128]{1,0:T(8,128)S(1)} collective-permute-done((f32[152,128]{1,0:T(8,128)S(1)}, f32[152,128]{1,0:T(8,128)S(1)}, u32[]{:S(2)}, u32[]{:S(2)}) %collective-permute-start.8) | collective-permute-done | bytes 77856 | tf_op jit(solution)/shard_map/ppermute | solution.py:122
  118.7 1.5 collective-permute-done.9
  120.6 1.2 collective-permute-start.12
  121.8 1.5 %collective-permute-start.13 = (f32[152,128]{1,0:T(8,128)S(1)}, f32[152,128]{1,0:T(8,128)S(1)}, u32[]{:S(2)}, u32[]{:S(2)}) collective-permute-start(f32[152,128]{1,0:T(8,128)S(1)} %add_add_fusion.1), channel_id=1, source_target_pairs={{0,48},{16,0},{32,16},{48,32},{1,49},{17,1},{33,17},{49,33},{2,50}... | collective-permute-start | bytes 233480 | tf_op jit(solution)/shard_map/ppermute | solution.py:122
  123.3 1.9 %collective-permute-done.11 = f32[152,128]{1,0:T(8,128)S(1)} collective-permute-done((f32[152,128]{1,0:T(8,128)S(1)}, f32[152,128]{1,0:T(8,128)S(1)}, u32[]{:S(2)}, u32[]{:S(2)}) %collective-permute-start.11) | collective-permute-done | bytes 77856 | tf_op jit(solution)/shard_map/ppermute | solution.py:122
  125.2 0.7 collective-permute-done.12
  125.9 6.2 %collective-permute-start.14 = (f32[152,128]{1,0:T(8,128)S(1)}, f32[152,128]{1,0:T(8,128)S(1)}, u32[]{:S(2)}, u32[]{:S(2)}) collective-permute-start(f32[152,128]{1,0:T(8,128)S(1)} %add_add_fusion), channel_id=1, source_target_pairs={{0,64},{64,128},{128,192},{192,0},{1,65},{65,129},{129,193},{193,1... | collective-permute-start | bytes 233480 | tf_op jit(solution)/shard_map/ppermute | solution.py:122
  132.1 0.5 collective-permute-start.16
  132.8 3.3 %copy.163 = bf16[1,1,2,4,4,4,512]{5,6,4,3,2,1,0:T(8,128)(2,1)} copy(bf16[1,1,2,4,4,4,512]{6,5,4,3,2,1,0:T(4,128)(2,1)S(1)} %reshape.277) | data formatting | bytes 262144 | tf_op jit(solution)/shard_map/reshape | solution.py:202
  136.1 9.7 %reshape.278 = bf16[1,1,2,16,2048]{4,3,2,1,0:T(8,128)(2,1)} reshape(bf16[1,1,2,4,4,512,4]{6,5,4,3,2,1,0:T(8,128)(2,1)} %bitcast.481) | data formatting | bytes 262144 | tf_op jit(solution)/shard_map/reshape | solution.py:205
  146.0 0.8 reshape.296
  146.8 0.8 reshape.297
  147.6 0.7 reshape.298
  (104 shorter events, 16.1 us)
Async XLA Ops:
  0.6 20.9 %copy-start = (bf16[16,64]{1,0:T(8,128)(2,1)S(1)}, bf16[16,64]{1,0:T(8,128)(2,1)}, u32[]{:S(2)}) copy-start(bf16[16,64]{1,0:T(8,128)(2,1)} %param.8) | copy-start | bytes 6148
  1.6 20.3 %collective-permute-start = (bf16[1,1,2,1,64,512]{5,4,3,2,1,0:T(8,128)(2,1)S(1)}, bf16[1,1,2,1,64,512]{5,4,3,2,1,0:T(8,128)(2,1)S(1)}, u32[]{:S(2)}, u32[]{:S(2)}) collective-permute-start(bf16[1,1,2,1,64,512]{5,4,3,2,1,0:T(8,128)(2,1)S(1)} %get-tuple-element.18), channel_id=1, source_target_pairs={{0,1},{1,2},{2,3},{3,4},{4,5},{5,6},{6,7},{7,8},{8,9},{9,10},{10,1... | collective-permute-start | bytes 393224 | tf_op jit(solution)/shard_map/ppermute | solution.py:18
  5.6 16.3 %collective-permute-start.1 = (bf16[1,1,2,1,64,512]{5,4,3,2,1,0:T(8,128)(2,1)S(1)}, bf16[1,1,2,1,64,512]{5,4,3,2,1,0:T(8,128)(2,1)S(1)}, u32[]{:S(2)}, u32[]{:S(2)}) collective-permute-start(bf16[1,1,2,1,64,512]{5,4,3,2,1,0:T(8,128)(2,1)S(1)} %get-tuple-element.19), channel_id=1, source_target_pairs={{1,0},{2,1},{3,2},{4,3},{5,4},{6,5},{7,6},{8,7},{9,8},{10,9},{11,1... | collective-permute-start | bytes 393224 | tf_op jit(solution)/shard_map/ppermute | solution.py:20
  17.7 4.2 %copy-start.1 = (bf16[1,1,2,4,64,512]{5,4,3,2,1,0:T(8,128)(2,1)S(1)}, bf16[1,1,2,4,64,512]{5,4,3,2,1,0:T(8,128)(2,1)}, u32[]{:S(2)}) copy-start(bf16[1,1,2,4,64,512]{5,4,3,2,1,0:T(8,128)(2,1)} %param.5) | copy-start | bytes 1572868
  23.5 1.3 copy-start.12
  24.7 1.9 %copy-start.4 = (bf16[2,4,64,512]{3,2,1,0:T(8,128)(2,1)}, bf16[2,4,64,512]{3,2,1,0:T(8,128)(2,1)S(1)}, u32[]{:S(2)}) copy-start(bf16[2,4,64,512]{3,2,1,0:T(8,128)(2,1)S(1)} %get-tuple-element.16) | copy-start | bytes 1572868
  29.0 12.2 %all-to-all-start = ((bf16[1,1,2,4,64,512]{5,4,2,1,0,3:T(8,128)(2,1)}), bf16[1,1,2,4,64,512]{5,4,2,1,0,3:T(8,128)(2,1)S(1)}, u32[]{:S(2)}, u32[]{:S(2)}) async-start(bf16[1,1,2,4,64,512]{5,4,2,1,0,3:T(8,128)(2,1)} %copy.160), calls=%async_computation | async-start | bytes 1048576 | tf_op jit(solution)/shard_map/all_to_all | solution.py:177
  34.0 10.8 %copy-start.3 = (bf16[3,3,64,64]{3,2,1,0:T(8,128)(2,1)S(1)}, bf16[3,3,64,64]{3,2,1,0:T(8,128)(2,1)}, u32[]{:S(2)}) copy-start(bf16[3,3,64,64]{3,2,1,0:T(8,128)(2,1)} %param.7) | copy-start | bytes 221188
  41.1 10.4 %all-to-all-start.2 = ((bf16[4,1,1,2,1,64,512]{6,5,3,4,2,1,0:T(8,128)(2,1)}), bf16[4,1,1,2,1,64,512]{6,5,3,4,2,1,0:T(8,128)(2,1)S(1)}, u32[]{:S(2)}, u32[]{:S(2)}) async-start(bf16[4,1,1,2,1,64,512]{6,5,3,4,2,1,0:T(8,128)(2,1)} %pad_maximum_fusion.2), calls=%async_computation.2 | async-start | bytes 1048576 | tf_op jit(solution)/shard_map/all_to_all | solution.py:192
  61.6 10.4 %all-to-all-start.3 = ((bf16[1,1,8,1,64,512]{5,4,3,1,0,2:T(8,128)(2,1)}), bf16[1,1,8,1,64,512]{5,4,3,1,0,2:T(8,128)(2,1)S(1)}, u32[]{:S(2)}, u32[]{:S(2)}) async-start(bf16[1,1,8,1,64,512]{5,4,3,1,0,2:T(8,128)(2,1)} %fusion.7), calls=%async_computation.3 | async-start | bytes 1048576 | tf_op jit(solution)/shard_map/all_to_all | solution.py:201
  65.5 10.0 %copy-start.2 = (f32[1,1,2,4,64,512]{5,4,3,2,1,0:T(8,128)S(1)}, f32[1,1,2,4,64,512]{5,4,3,2,1,0:T(8,128)}, u32[]{:S(2)}) copy-start(f32[1,1,2,4,64,512]{5,4,3,2,1,0:T(8,128)} %get-tuple-element.30) | copy-start | bytes 3145732
  72.0 10.4 %all-to-all-start.1 = ((bf16[1,1,8,1,64,512]{5,4,3,1,0,2:T(8,128)(2,1)}), bf16[1,1,8,1,64,512]{5,4,3,1,0,2:T(8,128)(2,1)S(1)}, u32[]{:S(2)}, u32[]{:S(2)}) async-start(bf16[1,1,8,1,64,512]{5,4,3,1,0,2:T(8,128)(2,1)} %get-tuple-element.5), calls=%async_computation.1 | async-start | bytes 1048576 | tf_op jit(solution)/shard_map/all_to_all | solution.py:183
  75.5 1.0 copy-start.5
  75.9 1.1 copy-start.11
  76.2 1.1 copy-start.10
  76.5 1.1 copy-start.9
  77.0 1.1 copy-start.8
  77.3 1.1 copy-start.7
  77.6 1.1 copy-start.6
  82.8 7.9 %collective-permute-start.2 = (f32[152,128]{1,0:T(8,128)S(1)}, f32[152,128]{1,0:T(8,128)S(1)}, u32[]{:S(2)}, u32[]{:S(2)}) collective-permute-start(f32[152,128]{1,0:T(8,128)S(1)} %get-tuple-element.28), channel_id=1, source_target_pairs={{0,128},{64,192},{128,0},{192,64},{1,129},{65,193},{129,1},{193,65... | collective-permute-start | bytes 233480 | tf_op jit(solution)/shard_map/ppermute | solution.py:122
  84.5 7.6 %collective-permute-start.3 = (f32[152,128]{1,0:T(8,128)S(1)}, f32[152,128]{1,0:T(8,128)S(1)}, u32[]{:S(2)}, u32[]{:S(2)}) collective-permute-start(f32[152,128]{1,0:T(8,128)S(1)} %get-tuple-element.27), channel_id=1, source_target_pairs={{0,64},{64,128},{128,192},{192,0},{1,65},{65,129},{129,193},{193,1... | collective-permute-start | bytes 233480 | tf_op jit(solution)/shard_map/ppermute | solution.py:122
  90.4 4.3 %collective-permute-start.4 = (f32[152,128]{1,0:T(8,128)S(1)}, f32[152,128]{1,0:T(8,128)S(1)}, u32[]{:S(2)}, u32[]{:S(2)}) collective-permute-start(f32[152,128]{1,0:T(8,128)S(1)} %get-tuple-element.26), channel_id=1, source_target_pairs={{0,192},{64,0},{128,64},{192,128},{1,193},{65,1},{129,65},{193,129... | collective-permute-start | bytes 233480 | tf_op jit(solution)/shard_map/ppermute | solution.py:122
  94.7 6.4 %collective-permute-start.5 = (f32[152,128]{1,0:T(8,128)S(1)}, f32[152,128]{1,0:T(8,128)S(1)}, u32[]{:S(2)}, u32[]{:S(2)}) collective-permute-start(f32[152,128]{1,0:T(8,128)S(1)} %fusion.85), channel_id=1, source_target_pairs={{0,2},{1,3},{2,0},{3,1},{4,6},{5,7},{6,4},{7,5},{8,10},{9,11},{10,... | collective-permute-start | bytes 233480 | tf_op jit(solution)/shard_map/ppermute | solution.py:122
  98.3 4.5 %collective-permute-start.6 = (f32[152,128]{1,0:T(8,128)S(1)}, f32[152,128]{1,0:T(8,128)S(1)}, u32[]{:S(2)}, u32[]{:S(2)}) collective-permute-start(f32[152,128]{1,0:T(8,128)S(1)} %fusion.85), channel_id=1, source_target_pairs={{0,1},{1,2},{2,3},{3,0},{4,5},{5,6},{6,7},{7,4},{8,9},{9,10},{10,1... | collective-permute-start | bytes 233480 | tf_op jit(solution)/shard_map/ppermute | solution.py:122
  100.1 3.7 %collective-permute-start.7 = (f32[152,128]{1,0:T(8,128)S(1)}, f32[152,128]{1,0:T(8,128)S(1)}, u32[]{:S(2)}, u32[]{:S(2)}) collective-permute-start(f32[152,128]{1,0:T(8,128)S(1)} %fusion.85), channel_id=1, source_target_pairs={{0,3},{1,0},{2,1},{3,2},{4,7},{5,4},{6,5},{7,6},{8,11},{9,8},{10,9... | collective-permute-start | bytes 233480 | tf_op jit(solution)/shard_map/ppermute | solution.py:122
  103.9 12.0 %collective-permute-start.10 = (f32[152,128]{1,0:T(8,128)S(1)}, f32[152,128]{1,0:T(8,128)S(1)}, u32[]{:S(2)}, u32[]{:S(2)}) collective-permute-start(f32[152,128]{1,0:T(8,128)S(1)} %add_add_fusion.2), channel_id=1, source_target_pairs={{0,12},{4,0},{8,4},{12,8},{1,13},{5,1},{9,5},{13,9},{2,14},{6,2},{... | collective-permute-start | bytes 233480 | tf_op jit(solution)/shard_map/ppermute | solution.py:122
  111.4 7.3 %collective-permute-start.8 = (f32[152,128]{1,0:T(8,128)S(1)}, f32[152,128]{1,0:T(8,128)S(1)}, u32[]{:S(2)}, u32[]{:S(2)}) collective-permute-start(f32[152,128]{1,0:T(8,128)S(1)} %add_add_fusion.2), channel_id=1, source_target_pairs={{0,8},{4,12},{8,0},{12,4},{1,9},{5,13},{9,1},{13,5},{2,10},{6,14},... | collective-permute-start | bytes 233480 | tf_op jit(solution)/shard_map/ppermute | solution.py:122
  113.6 6.6 %collective-permute-start.9 = (f32[152,128]{1,0:T(8,128)S(1)}, f32[152,128]{1,0:T(8,128)S(1)}, u32[]{:S(2)}, u32[]{:S(2)}) collective-permute-start(f32[152,128]{1,0:T(8,128)S(1)} %add_add_fusion.2), channel_id=1, source_target_pairs={{0,4},{4,8},{8,12},{12,0},{1,5},{5,9},{9,13},{13,1},{2,6},{6,10},{... | collective-permute-start | bytes 233480 | tf_op jit(solution)/shard_map/ppermute | solution.py:122
  120.2 4.9 %collective-permute-start.11 = (f32[152,128]{1,0:T(8,128)S(1)}, f32[152,128]{1,0:T(8,128)S(1)}, u32[]{:S(2)}, u32[]{:S(2)}) collective-permute-start(f32[152,128]{1,0:T(8,128)S(1)} %add_add_fusion.1), channel_id=1, source_target_pairs={{0,32},{16,48},{32,0},{48,16},{1,33},{17,49},{33,1},{49,17},{2,34}... | collective-permute-start | bytes 233480 | tf_op jit(solution)/shard_map/ppermute | solution.py:122
  120.6 5.3 %collective-permute-start.12 = (f32[152,128]{1,0:T(8,128)S(1)}, f32[152,128]{1,0:T(8,128)S(1)}, u32[]{:S(2)}, u32[]{:S(2)}) collective-permute-start(f32[152,128]{1,0:T(8,128)S(1)} %add_add_fusion.1), channel_id=1, source_target_pairs={{0,16},{16,32},{32,48},{48,0},{1,17},{17,33},{33,49},{49,1},{2,18}... | collective-permute-start | bytes 233480 | tf_op jit(solution)/shard_map/ppermute | solution.py:122
  121.8 4.1 %collective-permute-start.13 = (f32[152,128]{1,0:T(8,128)S(1)}, f32[152,128]{1,0:T(8,128)S(1)}, u32[]{:S(2)}, u32[]{:S(2)}) collective-permute-start(f32[152,128]{1,0:T(8,128)S(1)} %add_add_fusion.1), channel_id=1, source_target_pairs={{0,48},{16,0},{32,16},{48,32},{1,49},{17,1},{33,17},{49,33},{2,50}... | collective-permute-start | bytes 233480 | tf_op jit(solution)/shard_map/ppermute | solution.py:122
  125.9 19.9 %collective-permute-start.14 = (f32[152,128]{1,0:T(8,128)S(1)}, f32[152,128]{1,0:T(8,128)S(1)}, u32[]{:S(2)}, u32[]{:S(2)}) collective-permute-start(f32[152,128]{1,0:T(8,128)S(1)} %add_add_fusion), channel_id=1, source_target_pairs={{0,64},{64,128},{128,192},{192,0},{1,65},{65,129},{129,193},{193,1... | collective-permute-start | bytes 233480 | tf_op jit(solution)/shard_map/ppermute | solution.py:122
  132.1 13.8 %collective-permute-start.15 = (f32[152,128]{1,0:T(8,128)S(1)}, f32[152,128]{1,0:T(8,128)S(1)}, u32[]{:S(2)}, u32[]{:S(2)}) collective-permute-start(f32[152,128]{1,0:T(8,128)S(1)} %add_add_fusion), channel_id=1, source_target_pairs={{0,128},{64,192},{128,0},{192,64},{1,129},{65,193},{129,1},{193,65... | collective-permute-start | bytes 233480 | tf_op jit(solution)/shard_map/ppermute | solution.py:122
  132.1 13.8 %collective-permute-start.16 = (f32[152,128]{1,0:T(8,128)S(1)}, f32[152,128]{1,0:T(8,128)S(1)}, u32[]{:S(2)}, u32[]{:S(2)}) collective-permute-start(f32[152,128]{1,0:T(8,128)S(1)} %add_add_fusion), channel_id=1, source_target_pairs={{0,192},{64,0},{128,64},{192,128},{1,193},{65,1},{129,65},{193,129... | collective-permute-start | bytes 233480 | tf_op jit(solution)/shard_map/ppermute | solution.py:122
